TPU v7x, 256 devices: a whole 4x4x8 slice. The times are simulated.
256 devices in a mesh: section: 4 (over x), dp: 2 (over core), expert: 32 (over z, y).
Axes of the slice: x: 4, y: 4, z: 8, core: 2. Of those that a mesh axis runs over, the one named last changes fastest.
Arguments:
- tokens: bfloat16 [4, 8192, 2048], P('section', ('dp', 'expert')), may hold values from -6 to 6
- out_grad: bfloat16 [4, 8192, 2048], P('section', ('dp', 'expert')), may hold values from -6 to 6
- expert_ids: int32 [4, 8192, 2], P('section', ('dp', 'expert')), may hold values from 0 to 31, all different within a row; in each aligned block of 128 rows (0 to 127, 128 to 255, ..., all dimensions but the last counted through in order) at most 16 rows name the same one
- route_probs: float32 [4, 8192, 2], P('section', ('dp', 'expert')), may hold values from 0.1 to 1
- gate_weight: bfloat16 [4, 32, 2048, 768], P('section', 'expert', None, 'dp'), may hold values from -0.125 to 0.125
- up_weight: bfloat16 [4, 32, 2048, 768], P('section', 'expert', None, 'dp'), may hold values from -0.125 to 0.125
- down_weight: bfloat16 [4, 32, 768, 2048], P('section', 'expert', 'dp'), may hold values from -0.21875 to 0.21875
Outputs:
- grad_in: bfloat16 [4, 8192, 2048], P('section', ('dp', 'expert'))
- prob_grad: float32 [4, 8192, 2], P('section', ('dp', 'expert'))
- gate_weight_grad: bfloat16 [4, 32, 2048, 768], P('section', 'expert', None, 'dp')
- up_weight_grad: bfloat16 [4, 32, 2048, 768], P('section', 'expert', None, 'dp')
- down_weight_grad: bfloat16 [4, 32, 768, 2048], P('section', 'expert', 'dp')
Inputs may be any that keep to these rules, and one draw needn't show every extreme that they name: `expert_ids`: each token names 2 different experts; among the 128 tokens of one device (aligned blocks of 128 tokens of a section) no expert is named more than 16 times, a bound that some block reaches.
All inputs are finite; a program needn't handle non-finite values.
Results may differ from a plain program's by a relative error of at most 0.023.
Values may be sent and summed in bfloat16 or wider, within the bound.
A program may use at most 128 MiB of HBM per device.

v0:
```python
import jax
import jax.numpy as jnp
from jax import lax
from jax.sharding import PartitionSpec as P


def from_behind(shard, axis, by):
    length = lax.axis_size(axis)
    return lax.ppermute(shard, axis, [(i, (i + by) % length) for i in range(length)])


def expert_grads(rows_in, grads_in, weights_in, gate_part, up_part, down_part):
    contract_last = (((1,), (1,)), ((), ()))
    contract_first = (((0,), (0,)), ((), ()))
    gate_pre = jnp.dot(rows_in, gate_part, preferred_element_type=jnp.float32)
    up_pre = jnp.dot(rows_in, up_part, preferred_element_type=jnp.float32)
    sigmoid_gate = jax.nn.sigmoid(gate_pre)
    activated = gate_pre * sigmoid_gate * up_pre
    scaled_act = (weights_in[:, None] * activated).astype(jnp.bfloat16)
    hidden_grad = lax.dot_general(
        grads_in, down_part, contract_last, preferred_element_type=jnp.float32
    )
    prob_part = jnp.sum(activated * hidden_grad, axis=1)
    hidden_scaled = weights_in[:, None] * hidden_grad
    gate_grad = (
        hidden_scaled * up_pre * sigmoid_gate * (1.0 + gate_pre * (1.0 - sigmoid_gate))
    ).astype(jnp.bfloat16)
    up_grad = (hidden_scaled * gate_pre * sigmoid_gate).astype(jnp.bfloat16)
    route_dx = lax.dot_general(
        gate_grad, gate_part, contract_last, preferred_element_type=jnp.float32
    ) + lax.dot_general(up_grad, up_part, contract_last, preferred_element_type=jnp.float32)
    grad_gate = lax.dot_general(
        rows_in, gate_grad, contract_first, preferred_element_type=jnp.float32
    )
    grad_up = lax.dot_general(rows_in, up_grad, contract_first, preferred_element_type=jnp.float32)
    grad_down = lax.dot_general(
        scaled_act, grads_in, contract_first, preferred_element_type=jnp.float32
    )
    return (route_dx, prob_part, grad_gate, grad_up, grad_down)


def per_device(tokens, out_grad, expert_ids, route_probs, gate_weight, up_weight, down_weight):
    local_tokens = tokens[0]
    local_grads = out_grad[0]
    tok_count, row_width = local_tokens.shape
    top_count = expert_ids.shape[2]
    groups = lax.axis_size("expert")
    capacity = 2 * tok_count * top_count // groups
    slots_all = groups * capacity
    route_ids = expert_ids[0].reshape(-1)
    hit_table = (route_ids[:, None] == jnp.arange(groups, dtype=jnp.int32)[None, :]).astype(
        jnp.int32
    )
    before = jnp.cumsum(hit_table, axis=0) - hit_table
    slot_rank = jnp.sum(before * hit_table, axis=1)
    slot_of = route_ids * capacity + slot_rank
    placed = slot_of[None, :] == jnp.arange(slots_all, dtype=jnp.int32)[:, None]
    per_token = jnp.any(placed.reshape(slots_all, tok_count, top_count), axis=2).astype(
        jnp.bfloat16
    )
    send_rows = jnp.dot(per_token, local_tokens, preferred_element_type=jnp.float32).astype(
        jnp.bfloat16
    )
    send_grads = jnp.dot(per_token, local_grads, preferred_element_type=jnp.float32).astype(
        jnp.bfloat16
    )
    probs_flat = route_probs[0].reshape(-1)
    send_probs = jnp.sum(jnp.where(placed, probs_flat[None, :], 0.0), axis=1)
    recv_rows, recv_grads, recv_probs = (
        lax.all_to_all(
            send_rows.reshape(groups, capacity, row_width),
            "expert",
            split_axis=0,
            concat_axis=0,
            tiled=True,
        ),
        lax.all_to_all(
            send_grads.reshape(groups, capacity, row_width),
            "expert",
            split_axis=0,
            concat_axis=0,
            tiled=True,
        ),
        lax.all_to_all(
            send_probs.reshape(groups, capacity).astype(jnp.bfloat16),
            "expert",
            split_axis=0,
            concat_axis=0,
            tiled=True,
        ).astype(jnp.float32),
    )
    recv_rows = recv_rows.reshape(slots_all, row_width)
    recv_grads = recv_grads.reshape(slots_all, row_width)
    recv_probs = recv_probs.reshape(slots_all)
    gate_part = gate_weight[0, 0]
    up_part = up_weight[0, 0]
    down_part = down_weight[0, 0]
    gate_full, up_full, down_full = (
        lax.all_gather(gate_part, "dp", axis=1, tiled=True),
        lax.all_gather(up_part, "dp", axis=1, tiled=True),
        lax.all_gather(down_part, "dp", axis=0, tiled=True),
    )
    route_dx, prob_part, grad_gate, grad_up, grad_down = expert_grads(
        recv_rows, recv_grads, recv_probs, gate_full, up_full, down_full
    )
    grad_gate, grad_up, grad_down = (
        lax.psum_scatter(
            grad_gate.astype(jnp.bfloat16), "dp", scatter_dimension=1, tiled=True
        ).astype(jnp.float32),
        lax.psum_scatter(
            grad_up.astype(jnp.bfloat16), "dp", scatter_dimension=1, tiled=True
        ).astype(jnp.float32),
        lax.psum_scatter(
            grad_down.astype(jnp.bfloat16), "dp", scatter_dimension=0, tiled=True
        ).astype(jnp.float32),
    )
    back_rows, back_probs = (
        lax.all_to_all(
            route_dx.astype(jnp.bfloat16).reshape(groups, capacity, row_width),
            "expert",
            split_axis=0,
            concat_axis=0,
            tiled=True,
        ),
        lax.all_to_all(
            prob_part.reshape(groups, capacity).astype(jnp.bfloat16),
            "expert",
            split_axis=0,
            concat_axis=0,
            tiled=True,
        ).astype(jnp.float32),
    )
    token_grad = lax.dot_general(
        per_token,
        back_rows.reshape(slots_all, row_width),
        (((0,), (0,)), ((), ())),
        preferred_element_type=jnp.float32,
    ).astype(jnp.bfloat16)
    route_grad = jnp.sum(jnp.where(placed, back_probs.reshape(slots_all)[:, None], 0.0), axis=0)
    route_grad = route_grad.reshape(tok_count, top_count)
    upstream = from_behind(token_grad, "section", -1)
    return (
        upstream[None],
        route_grad[None],
        grad_gate.astype(jnp.bfloat16)[None, None],
        grad_up.astype(jnp.bfloat16)[None, None],
        grad_down.astype(jnp.bfloat16)[None, None],
    )


def solution(mesh):
    in_specs = (
        P("section", ("dp", "expert"), None),
        P("section", ("dp", "expert"), None),
        P("section", ("dp", "expert"), None),
        P("section", ("dp", "expert"), None),
        P("section", "expert", None, "dp"),
        P("section", "expert", None, "dp"),
        P("section", "expert", "dp", None),
    )
    out_specs = (
        P("section", ("dp", "expert"), None),
        P("section", ("dp", "expert"), None),
        P("section", "expert", None, "dp"),
        P("section", "expert", None, "dp"),
        P("section", "expert", "dp", None),
    )
    return jax.shard_map(
        per_device, mesh=mesh, in_specs=in_specs, out_specs=out_specs, check_vma=False
    )
```

profile of v0, /device:TPU:6, one launch (start us, length us, event | category | flops | bytes accessed | tf_op | source)
XLA Modules:
  0.0 274.5 jit_solution(8630525464374877536)
XLA Ops:
  7.9 0.8 copy.27
  10.2 2.0 convolution_convert_fusion.3
  12.3 11.6 %all-to-all-start.2 = ((bf16[32,16,2048]{2,1,0:T(8,128)(2,1)}), bf16[32,16,2048]{2,1,0:T(8,128)(2,1)S(1)}, u32[]{:S(2)}, u32[]{:S(2)}) async-start(bf16[32,16,2048]{2,1,0:T(8,128)(2,1)} %bitcast.7), calls=%async_computation.2 | async-start | bytes 4194304 | tf_op jit(solution)/shard_map/all_to_all | solution.py:70
  24.7 2.0 convolution_convert_fusion.4
  26.7 47.4 %all-to-all-done.2 = bf16[32,16,2048]{2,1,0:T(8,128)(2,1)S(1)} async-done(((bf16[32,16,2048]{2,1,0:T(8,128)(2,1)}), bf16[32,16,2048]{2,1,0:T(8,128)(2,1)S(1)}, u32[]{:S(2)}, u32[]{:S(2)}) %all-to-all-start.2) | async-done | bytes 2097184 | tf_op jit(solution)/shard_map/all_to_all | solution.py:70
  74.1 6.1 %all-to-all-start.1 = ((bf16[32,16,2048]{2,1,0:T(8,128)(2,1)}), bf16[32,16,2048]{2,1,0:T(8,128)(2,1)}, u32[]{:S(2)}, u32[]{:S(2)}) async-start(bf16[32,16,2048]{2,1,0:T(8,128)(2,1)} %bitcast.3), calls=%async_computation.1 | async-start | bytes 4194304 | tf_op jit(solution)/shard_map/all_to_all | solution.py:77
  80.9 4.8 %fusion.2 = f32[512,768]{1,0:T(8,128)} fusion(bf16[512,2048]{1,0:T(8,128)(2,1)S(1)} %bitcast.75, bf16[1,1,2048,768]{3,2,1,0:T(8,128)(2,1)} %all-gather.11.cloned.1.call-done), kind=kOutput, calls=%fused_computation.6 | convolution fusion | flops 1610612736 | bytes 6815744 | tf_op jit(solution)/shard_map/dot_general | solution.py:15
  85.7 4.8 %fusion.6 = f32[512,768]{1,0:T(8,128)} fusion(bf16[512,2048]{1,0:T(8,128)(2,1)S(1)} %bitcast.76, bf16[1,1,2048,768]{3,2,1,0:T(8,128)(2,1)} %all-gather.9.cloned.1.call-done), kind=kOutput, calls=%fused_computation.10 | convolution fusion | flops 1610612736 | bytes 6815744 | tf_op jit(solution)/shard_map/dot_general | solution.py:16
  90.6 10.8 %all-gather.7.cloned.1.call-done = bf16[1,1,768,2048]{3,2,1,0:T(8,128)(2,1)} async-done(((bf16[1,1,384,2048]{3,2,1,0:T(8,128)(2,1)}), bf16[1,1,768,2048]{3,2,1,0:T(8,128)(2,1)}) %all-gather.7.cloned.1.call-update) | async-done | bytes 3145744 | tf_op jit(solution)/shard_map/all_gather | solution.py:101
  101.4 27.9 %all-to-all-done.1 = bf16[32,16,2048]{2,1,0:T(8,128)(2,1)} async-done(((bf16[32,16,2048]{2,1,0:T(8,128)(2,1)}), bf16[32,16,2048]{2,1,0:T(8,128)(2,1)}, u32[]{:S(2)}, u32[]{:S(2)}) %all-to-all-start.1) | async-done | bytes 2097184 | tf_op jit(solution)/shard_map/all_to_all | solution.py:77
  129.3 6.5 %multiply_reduce_fusion = (bf16[512]{0:T(512)(128)(2,1)S(1)}, f32[512,768]{1,0:T(8,128)}) fusion(f32[512,768]{1,0:T(8,128)} %fusion.6, f32[512,768]{1,0:T(8,128)} %fusion.2, bf16[512,2048]{1,0:T(8,128)(2,1)} %bitcast.4, bf16[1,1,768,2048]{3,2,1,0:T(8,128)(2,1)} %all-gather.7.cloned.1.call-done), kind=kOutput, calls=%fused_computation.18 | convolution fusion | flops 1613364736 | bytes 9962496 | tf_op jit(solution)/shard_map/dot_general | solution.py:20
  135.7 0.7 convert_element_type.113
  136.4 5.9 %all-to-all-start.4 = ((bf16[32,1,16]{2,1,0:T(2,128)(2,1)}), bf16[32,1,16]{2,1,0:T(2,128)(2,1)S(1)}, u32[]{:S(2)}, u32[]{:S(2)}) async-start(bf16[32,1,16]{2,1,0:T(2,128)(2,1)} %convert_element_type.113), calls=%async_computation.4 | async-start | bytes 32768 | tf_op jit(solution)/shard_map/all_to_all | solution.py:125
  142.7 9.3 %all-to-all-done.4 = bf16[32,1,16]{2,1,0:T(2,128)(2,1)S(1)} async-done(((bf16[32,1,16]{2,1,0:T(2,128)(2,1)}), bf16[32,1,16]{2,1,0:T(2,128)(2,1)S(1)}, u32[]{:S(2)}, u32[]{:S(2)}) %all-to-all-start.4) | async-done | bytes 1056 | tf_op jit(solution)/shard_map/all_to_all | solution.py:125
  152.5 12.7 %all_to_all.27 = bf16[32,1,16]{2,1,0:T(2,128)(2,1)S(1)} all-to-all(bf16[32,1,16]{2,1,0:T(2,128)(2,1)S(1)} %convert_element_type.112), channel_id=1, replica_groups=mesh['section'=4,'dp'=2,'expert'=32] {'expert'}, dimensions={0} | all-to-all | bytes 2048 | tf_op jit(solution)/shard_map/all_to_all | solution.py:84
  165.4 3.1 %multiply_convert_fusion.1 = (bf16[512,768]{1,0:T(8,128)(2,1)S(1)}, bf16[512,768]{1,0:T(8,128)(2,1)S(1)}) fusion(f32[512,768]{1,0:T(8,128)} %fusion.2, f32[512,768]{1,0:T(8,128)} %get-tuple-element.25, f32[512]{0:T(512)S(1)} %reshape.116, f32[512,768]{1,0:T(8,128)} %fusion.6), kind=kLoop, calls=%fused_computation.20 | loop fusion | flops 5505024 | bytes 6293504 | tf_op jit(solution)/shard_map/convert_element_type | solution.py:28
  168.5 0.9 copy-done.2
  169.4 3.5 %convolution_convert_fusion.2 = bf16[2048,768]{1,0:T(8,128)(2,1)} fusion(bf16[512,2048]{1,0:T(8,128)(2,1)S(1)} %bitcast.77, bf16[512,768]{1,0:T(8,128)(2,1)S(1)} %get-tuple-element.23), kind=kOutput, calls=%fused_computation.3 | convolution fusion | flops 1612185600 | bytes 6029312 | tf_op jit(solution)/shard_map/dot_general | solution.py:32
  172.8 4.8 %copy.36 = bf16[2048,768]{0,1:T(8,128)(2,1)} copy(bf16[2048,768]{1,0:T(8,128)(2,1)} %convolution_convert_fusion.2) | data formatting | bytes 6291456
  177.7 3.5 %convolution_convert_fusion.1 = bf16[2048,768]{1,0:T(8,128)(2,1)} fusion(bf16[512,2048]{1,0:T(8,128)(2,1)S(1)} %bitcast.78, bf16[512,768]{1,0:T(8,128)(2,1)S(1)} %get-tuple-element.22), kind=kOutput, calls=%fused_computation.2 | convolution fusion | flops 1612185600 | bytes 6029312 | tf_op jit(solution)/shard_map/dot_general | solution.py:35
  181.2 4.9 %copy.38 = bf16[2048,768]{0,1:T(8,128)(2,1)} copy(bf16[2048,768]{1,0:T(8,128)(2,1)} %convolution_convert_fusion.1) | data formatting | bytes 6291456
  186.2 1.4 copy-done.1
  187.6 5.8 %convolution_convert_fusion = bf16[768,2048]{1,0:T(8,128)(2,1)} fusion(bf16[512,2048]{1,0:T(8,128)(2,1)} %bitcast.4, f32[512]{0:T(512)S(1)} %reshape.116, f32[512,768]{1,0:T(8,128)} %fusion.6, f32[512,768]{1,0:T(8,128)S(1)} %copy-done.1), kind=kOutput, calls=%fused_computation.1 | convolution fusion | flops 1614938112 | bytes 8390656 | tf_op jit(solution)/shard_map/dot_general | solution.py:36
  193.4 1.1 copy-done.3
  194.6 3.9 %fusion = f32[512,2048]{1,0:T(8,128)S(1)} fusion(bf16[512,768]{1,0:T(8,128)(2,1)S(1)} %copy-done.3, bf16[1,1,2048,768]{3,2,1,0:T(8,128)(2,1)} %all-gather.11.cloned.1.call-done), kind=kOutput, calls=%fused_computation.4 | convolution fusion | flops 1610612736 | bytes 8126464 | tf_op jit(solution)/shard_map/dot_general | solution.py:29
  198.4 1.8 add_convert_fusion
  200.3 50.4 %all_to_all.28 = bf16[32,16,2048]{2,1,0:T(8,128)(2,1)S(1)} all-to-all(bf16[32,16,2048]{2,1,0:T(8,128)(2,1)S(1)} %bitcast.79), channel_id=1, replica_groups=mesh['section'=4,'dp'=2,'expert'=32] {'expert'}, dimensions={0} | all-to-all | bytes 4194304 | tf_op jit(solution)/shard_map/all_to_all | solution.py:118
  251.2 0.9 collective-permute-start
  252.9 8.8 %collective-permute-done = bf16[128,2048]{1,0:T(8,128)(2,1)S(1)} collective-permute-done((bf16[128,2048]{1,0:T(8,128)(2,1)S(1)}, bf16[128,2048]{1,0:T(8,128)(2,1)S(1)}, u32[]{:S(2)}, u32[]{:S(2)}) %collective-permute-start) | collective-permute-done | bytes 524320 | tf_op jit(solution)/shard_map/ppermute | solution.py:9
  261.7 2.6 copy.37
  264.3 2.6 copy.39
  266.8 0.8 copy.43
  (52 shorter events, 6.0 us)
Async XLA Ops:
  7.2 3.1 %copy-start = (bf16[1,128,2048]{2,1,0:T(8,128)(2,1)S(1)}, bf16[1,128,2048]{2,1,0:T(8,128)(2,1)}, u32[]{:S(2)}) copy-start(bf16[1,128,2048]{2,1,0:T(8,128)(2,1)} %param.7) | copy-start | bytes 1572868
  7.2 73.7 %all-gather.11.cloned.1.call-start = ((), (), s32[]{:S(2)}) async-start(), calls=%async_computation.11 | async-start | bytes 4718592 | tf_op jit(solution)/shard_map/all_gather | solution.py:99
  12.3 12.4 %copy-start.4 = (bf16[1,128,2048]{2,1,0:T(8,128)(2,1)S(1)}, bf16[1,128,2048]{2,1,0:T(8,128)(2,1)}, u32[]{:S(2)}) copy-start(bf16[1,128,2048]{2,1,0:T(8,128)(2,1)} %param.8) | copy-start | bytes 1572868
  12.3 61.8 %all-to-all-start.2 = ((bf16[32,16,2048]{2,1,0:T(8,128)(2,1)}), bf16[32,16,2048]{2,1,0:T(8,128)(2,1)S(1)}, u32[]{:S(2)}, u32[]{:S(2)}) async-start(bf16[32,16,2048]{2,1,0:T(8,128)(2,1)} %bitcast.7), calls=%async_computation.2 | async-start | bytes 4194304 | tf_op jit(solution)/shard_map/all_to_all | solution.py:70
  23.9 61.8 %all-gather.9.cloned.1.call-start = ((), (), s32[]{:S(2)}) async-start(), calls=%async_computation.10 | async-start | bytes 4718592 | tf_op jit(solution)/shard_map/all_gather | solution.py:100
  74.1 55.2 %all-to-all-start.1 = ((bf16[32,16,2048]{2,1,0:T(8,128)(2,1)}), bf16[32,16,2048]{2,1,0:T(8,128)(2,1)}, u32[]{:S(2)}, u32[]{:S(2)}) async-start(bf16[32,16,2048]{2,1,0:T(8,128)(2,1)} %bitcast.3), calls=%async_computation.1 | async-start | bytes 4194304 | tf_op jit(solution)/shard_map/all_to_all | solution.py:77
  80.1 21.3 %all-gather.7.cloned.1.call-start = ((), (), s32[]{:S(2)}) async-start(), calls=%async_computation.9 | async-start | bytes 4718592 | tf_op jit(solution)/shard_map/all_gather | solution.py:101
  129.3 13.2 %copy-start.5 = (f32[1,128,2]{1,2,0:T(2,128)S(1)}, f32[1,128,2]{1,2,0:T(2,128)}, u32[]{:S(2)}) copy-start(f32[1,128,2]{1,2,0:T(2,128)} %param.10) | copy-start | bytes 3076
  136.4 15.6 %all-to-all-start.4 = ((bf16[32,1,16]{2,1,0:T(2,128)(2,1)}), bf16[32,1,16]{2,1,0:T(2,128)(2,1)S(1)}, u32[]{:S(2)}, u32[]{:S(2)}) async-start(bf16[32,1,16]{2,1,0:T(2,128)(2,1)} %convert_element_type.113), calls=%async_computation.4 | async-start | bytes 32768 | tf_op jit(solution)/shard_map/all_to_all | solution.py:125
  142.4 119.3 %reduce-scatter.10.cloned.1.call-start = ((), (), s32[]{:S(2)}) async-start(), calls=%async_computation.12 | async-start | bytes 4718592
  168.5 0.9 copy-start.2
  177.6 86.6 %reduce-scatter.12.cloned.1.call-start = ((), (), s32[]{:S(2)}) async-start(), calls=%async_computation.13 | async-start | bytes 4718592
  186.1 1.5 copy-start.1
  186.1 80.7 %reduce-scatter.8.cloned.1.call-start = ((), (), s32[]{:S(2)}) async-start(), calls=%async_computation.8 | async-start | bytes 4718592 | tf_op jit(solution)/shard_map/reduce_scatter | solution.py:113
  193.4 1.1 copy-start.3
  194.6 3.9 %copy-start.6 = (bf16[1,1,2048,768]{3,2,1,0:T(8,128)(2,1)S(1)}, bf16[1,1,2048,768]{3,2,1,0:T(8,128)(2,1)}, u32[]{:S(2)}) copy-start(bf16[1,1,2048,768]{3,2,1,0:T(8,128)(2,1)} %all-gather.9.cloned.1.call-done) | copy-start | bytes 9437188
  251.2 10.5 %collective-permute-start = (bf16[128,2048]{1,0:T(8,128)(2,1)S(1)}, bf16[128,2048]{1,0:T(8,128)(2,1)S(1)}, u32[]{:S(2)}, u32[]{:S(2)}) collective-permute-start(bf16[128,2048]{1,0:T(8,128)(2,1)S(1)} %convolution_convert_fusion.5), channel_id=1, source_target_pairs={{0,192},{64,0},{128,64},{192,128},{1,193},{65,1},{129,65},{193,129... | collective-permute-start | bytes 1572872 | tf_op jit(solution)/shard_map/ppermute | solution.py:9
Sparse Core Ops, SparseCore 0:
  9.8 20.2 all-gather.10
  31.9 18.6 all-gather.8
  82.8 18.5 all-gather.6
  177.7 10.6 reduce-scatter.9
  190.9 17.4 reduce-scatter.11
  211.4 17.5 reduce-scatter.7
where the time goes:
time: 275 us; the launch traced here: 274 us
  waiting for transfers between devices  106 us (39%)
  blocking collectives  63.1 us (23%)
  matrix products  39.1 us (14%)
  starting transfers between devices  24.8 us (9%)
  local copies, waits for them, and re-layouts  22.5 us (8%)
  between operations  14.3 us (5%)
  other arithmetic  4.3 us (2%)
    all_to_all x1, blocking collectives, per_device(): lax.all_to_all(route_dx.astype(jnp.bfloat16).reshape(groups, capacity, ro...  50.4 us
    all_to_all x1, waiting for transfers between devices, per_device(): lax.all_to_all(send_rows.reshape(groups, capacity, row_width), 'expert',...  47.4 us
    all_to_all x1, waiting for transfers between devices, per_device(): lax.all_to_all(send_grads.reshape(groups, capacity, row_width), 'expert',...  27.9 us
    unnamed x22, local copies, waits for them, and re-layouts  20.6 us
    all_to_all x1, blocking collectives, per_device(): lax.all_to_all(send_probs.reshape(groups, capacity).astype(jnp.bfloat16),...  12.7 us
    all_to_all x1, starting transfers between devices, per_device(): lax.all_to_all(send_rows.reshape(groups, capacity, row_width), 'expert',...  11.6 us
    all_gather x1, waiting for transfers between devices, per_device(): lax.all_gather(down_part, 'dp', axis=0, tiled=True)  10.8 us
    all_to_all x1, waiting for transfers between devices, per_device(): lax.all_to_all(prob_part.reshape(groups, capacity).astype(jnp.bfloat16),...  9.33 us
  transfers between devices with their start and end apart: 10, of which 5 were waited for; matrix products, arithmetic and copies ran while one was open for 16% of the time, Pallas kernels for 0%

commit v1 on v0

--- a/solution.py
+++ b/solution.py
@@ -98,7 +98,9 @@
     gate_full, up_full, down_full = (
         lax.all_gather(gate_part, "dp", axis=1, tiled=True),
         lax.all_gather(up_part, "dp", axis=1, tiled=True),
-        lax.all_gather(down_part, "dp", axis=0, tiled=True),
+        jnp.concatenate(
+            lax.all_to_all(jnp.stack([down_part] * lax.axis_size("dp")), "dp", 0, 0), axis=0
+        ),
     )
     route_dx, prob_part, grad_gate, grad_up, grad_down = expert_grads(
         recv_rows, recv_grads, recv_probs, gate_full, up_full, down_full

time: 275 us -> 285 us (1.036)
  starting transfers between devices: 24.8 us -> 30.1 us
  other arithmetic: 4.3 us -> 9.11 us
    all_gather x1, waiting for transfers between devices: 0.01 us -> 15.6 us  [per_device(): lax.all_gather(up_part, 'dp', axis=1, tiled=True)]
    all_gather x1 -> x0, waiting for transfers between devices: 10.8 us -> none  [per_device(): lax.all_gather(down_part, 'dp', axis=0, tiled=True)]
    all_to_all x0 -> x1, starting transfers between devices: none -> 5.32 us  [per_device(): lax.all_to_all(jnp.stack([down_part] * lax.axis_size('dp')), 'dp', 0, 0)]
    all_to_all x1, waiting for transfers between devices: 27.9 us -> 23.8 us  [per_device(): lax.all_to_all(send_grads.reshape(groups, capacity, row_width), 'expert',...]
    another operation x2 -> x3, other arithmetic: 0.63 us -> 4.56 us  [the longest x1 3.93 us: per_device(): jnp.stack([down_part] * lax.axis_size('dp'))]
    unnamed x22 -> x24, local copies, waits for them, and re-layouts: 20.6 us -> 19 us
  transfers between devices with their start and end apart: 10 -> 10, of which waited for: 5 -> 5; matrix products, arithmetic and copies ran while one was open for 16% -> 15% of each run, Pallas kernels for 0% -> 0%
where the time goes in v1:
time: 285 us; the launch traced here: 284 us
  waiting for transfers between devices  107 us (38%)
  blocking collectives  63.1 us (22%)
  matrix products  40.2 us (14%)
  starting transfers between devices  30.1 us (11%)
  local copies, waits for them, and re-layouts  20.9 us (7%)
  between operations  14 us (5%)
  other arithmetic  9.11 us (3%)
    all_to_all x1, blocking collectives, per_device(): lax.all_to_all(route_dx.astype(jnp.bfloat16).reshape(groups, capacity, ro...  50.4 us
    all_to_all x1, waiting for transfers between devices, per_device(): lax.all_to_all(send_rows.reshape(groups, capacity, row_width), 'expert',...  48 us
    all_to_all x1, waiting for transfers between devices, per_device(): lax.all_to_all(send_grads.reshape(groups, capacity, row_width), 'expert',...  23.8 us
    unnamed x24, local copies, waits for them, and re-layouts  19 us
    all_gather x1, waiting for transfers between devices, per_device(): lax.all_gather(up_part, 'dp', axis=1, tiled=True)  15.6 us
    all_to_all x1, blocking collectives, per_device(): lax.all_to_all(send_probs.reshape(groups, capacity).astype(jnp.bfloat16),...  12.7 us
    all_to_all x1, starting transfers between devices, per_device(): lax.all_to_all(send_rows.reshape(groups, capacity, row_width), 'expert',...  11.6 us
    all_to_all x1, waiting for transfers between devices, per_device(): lax.all_to_all(prob_part.reshape(groups, capacity).astype(jnp.bfloat16),...  9.33 us
  transfers between devices with their start and end apart: 10, of which 5 were waited for; matrix products, arithmetic and copies ran while one was open for 15% of the time, Pallas kernels for 0%

profile of v1, /device:TPU:6, one launch (start us, length us, event | category | flops | bytes accessed | tf_op | source)
XLA Modules:
  0.0 284.3 jit_solution(2692629110328732722)
XLA Ops:
  7.2 3.9 %pad_maximum_fusion = bf16[2,384,2048]{2,1,0:T(8,128)(2,1)} fusion(bf16[1,384,2048]{2,1,0:T(8,128)(2,1)} %bitcast.82), kind=kLoop, calls=%fused_computation.4 | loop fusion | flops 1572864 | bytes 4718592 | tf_op jit(solution)/shard_map/stack | solution.py:102
  11.1 5.3 %all-to-all-start.2 = ((bf16[2,384,2048]{2,1,0:T(8,128)(2,1)}), bf16[2,384,2048]{2,1,0:T(8,128)(2,1)}, u32[]{:S(2)}, u32[]{:S(2)}) async-start(bf16[2,384,2048]{2,1,0:T(8,128)(2,1)} %pad_maximum_fusion), calls=%async_computation.2 | async-start | bytes 6291456 | tf_op jit(solution)/shard_map/all_to_all | solution.py:102
  18.1 2.1 convolution_convert_fusion.3
  20.2 11.6 %all-to-all-start.3 = ((bf16[32,16,2048]{2,1,0:T(8,128)(2,1)}), bf16[32,16,2048]{2,1,0:T(8,128)(2,1)S(1)}, u32[]{:S(2)}, u32[]{:S(2)}) async-start(bf16[32,16,2048]{2,1,0:T(8,128)(2,1)} %bitcast.8), calls=%async_computation.3 | async-start | bytes 4194304 | tf_op jit(solution)/shard_map/all_to_all | solution.py:70
  32.6 2.0 convolution_convert_fusion.4
  34.6 48.0 %all-to-all-done.3 = bf16[32,16,2048]{2,1,0:T(8,128)(2,1)S(1)} async-done(((bf16[32,16,2048]{2,1,0:T(8,128)(2,1)}), bf16[32,16,2048]{2,1,0:T(8,128)(2,1)S(1)}, u32[]{:S(2)}, u32[]{:S(2)}) %all-to-all-start.3) | async-done | bytes 2097184 | tf_op jit(solution)/shard_map/all_to_all | solution.py:70
  82.6 6.1 %all-to-all-start.1 = ((bf16[32,16,2048]{2,1,0:T(8,128)(2,1)}), bf16[32,16,2048]{2,1,0:T(8,128)(2,1)}, u32[]{:S(2)}, u32[]{:S(2)}) async-start(bf16[32,16,2048]{2,1,0:T(8,128)(2,1)} %bitcast.3), calls=%async_computation.1 | async-start | bytes 4194304 | tf_op jit(solution)/shard_map/all_to_all | solution.py:77
  89.5 4.8 %fusion.2 = f32[512,768]{1,0:T(8,128)} fusion(bf16[512,2048]{1,0:T(8,128)(2,1)S(1)} %bitcast.73, bf16[1,1,2048,768]{3,2,1,0:T(8,128)(2,1)} %all-gather.7.cloned.1.call-done), kind=kOutput, calls=%fused_computation.7 | convolution fusion | flops 1610612736 | bytes 6815744 | tf_op jit(solution)/shard_map/dot_general | solution.py:15
  94.3 15.6 %all-gather.5.cloned.1.call-done = bf16[1,1,2048,768]{3,2,1,0:T(8,128)(2,1)} async-done(((bf16[1,1,2048,384]{3,2,1,0:T(8,128)(2,1)}), bf16[1,1,2048,768]{3,2,1,0:T(8,128)(2,1)}) %all-gather.5.cloned.1.call-update) | async-done | bytes 3145744 | tf_op jit(solution)/shard_map/all_gather | solution.py:100
  109.9 4.8 %fusion.6 = f32[512,768]{1,0:T(8,128)} fusion(bf16[512,2048]{1,0:T(8,128)(2,1)S(1)} %bitcast.74, bf16[1,1,2048,768]{3,2,1,0:T(8,128)(2,1)} %all-gather.5.cloned.1.call-done), kind=kOutput, calls=%fused_computation.11 | convolution fusion | flops 1610612736 | bytes 6815744 | tf_op jit(solution)/shard_map/dot_general | solution.py:16
  114.7 23.8 %all-to-all-done.1 = bf16[32,16,2048]{2,1,0:T(8,128)(2,1)} async-done(((bf16[32,16,2048]{2,1,0:T(8,128)(2,1)}), bf16[32,16,2048]{2,1,0:T(8,128)(2,1)}, u32[]{:S(2)}, u32[]{:S(2)}) %all-to-all-start.1) | async-done | bytes 2097184 | tf_op jit(solution)/shard_map/all_to_all | solution.py:77
  138.5 6.5 %multiply_reduce_fusion = (bf16[512]{0:T(512)(128)(2,1)S(1)}, f32[512,768]{1,0:T(8,128)}) fusion(f32[512,768]{1,0:T(8,128)} %fusion.6, f32[512,768]{1,0:T(8,128)} %fusion.2, bf16[512,2048]{1,0:T(8,128)(2,1)} %bitcast.4, bf16[768,2048]{1,0:T(8,128)(2,1)} %bitcast.6), kind=kOutput, calls=%fused_computation.17 | convolution fusion | flops 1613364736 | bytes 9962496 | tf_op jit(solution)/shard_map/dot_general | solution.py:20
  145.0 0.7 convert_element_type.113
  145.7 5.9 %all-to-all-start.5 = ((bf16[32,1,16]{2,1,0:T(2,128)(2,1)}), bf16[32,1,16]{2,1,0:T(2,128)(2,1)S(1)}, u32[]{:S(2)}, u32[]{:S(2)}) async-start(bf16[32,1,16]{2,1,0:T(2,128)(2,1)} %convert_element_type.113), calls=%async_computation.5 | async-start | bytes 32768 | tf_op jit(solution)/shard_map/all_to_all | solution.py:127
  151.9 9.3 %all-to-all-done.5 = bf16[32,1,16]{2,1,0:T(2,128)(2,1)S(1)} async-done(((bf16[32,1,16]{2,1,0:T(2,128)(2,1)}), bf16[32,1,16]{2,1,0:T(2,128)(2,1)S(1)}, u32[]{:S(2)}, u32[]{:S(2)}) %all-to-all-start.5) | async-done | bytes 1056 | tf_op jit(solution)/shard_map/all_to_all | solution.py:127
  161.7 12.7 %all_to_all.32 = bf16[32,1,16]{2,1,0:T(2,128)(2,1)S(1)} all-to-all(bf16[32,1,16]{2,1,0:T(2,128)(2,1)S(1)} %convert_element_type.112), channel_id=1, replica_groups=mesh['section'=4,'dp'=2,'expert'=32] {'expert'}, dimensions={0} | all-to-all | bytes 2048 | tf_op jit(solution)/shard_map/all_to_all | solution.py:84
  174.6 4.0 %multiply_convert_fusion.1 = (bf16[512,768]{1,0:T(8,128)(2,1)S(1)}, bf16[512,768]{1,0:T(8,128)(2,1)}) fusion(f32[512,768]{1,0:T(8,128)} %fusion.2, f32[512,768]{1,0:T(8,128)} %get-tuple-element.25, f32[512]{0:T(512)S(1)} %reshape.120, f32[512,768]{1,0:T(8,128)} %fusion.6), kind=kLoop, calls=%fused_computation.19 | loop fusion | flops 5505024 | bytes 6293504 | tf_op jit(solution)/shard_map/convert_element_type | solution.py:28
  178.6 3.5 %convolution_convert_fusion.1 = bf16[2048,768]{1,0:T(8,128)(2,1)} fusion(bf16[512,2048]{1,0:T(8,128)(2,1)S(1)} %bitcast.75, bf16[512,768]{1,0:T(8,128)(2,1)S(1)} %get-tuple-element.22), kind=kOutput, calls=%fused_computation.2 | convolution fusion | flops 1612185600 | bytes 6029312 | tf_op jit(solution)/shard_map/dot_general | solution.py:35
  182.0 4.8 %copy.38 = bf16[2048,768]{0,1:T(8,128)(2,1)} copy(bf16[2048,768]{1,0:T(8,128)(2,1)} %convolution_convert_fusion.1) | data formatting | bytes 6291456
  186.9 4.6 %convolution_convert_fusion.2 = bf16[2048,768]{1,0:T(8,128)(2,1)} fusion(bf16[512,2048]{1,0:T(8,128)(2,1)S(1)} %bitcast.76, bf16[512,768]{1,0:T(8,128)(2,1)} %get-tuple-element.23), kind=kOutput, calls=%fused_computation.3 | convolution fusion | flops 1612185600 | bytes 6029312 | tf_op jit(solution)/shard_map/dot_general | solution.py:32
  191.5 4.8 %copy.36 = bf16[2048,768]{0,1:T(8,128)(2,1)} copy(bf16[2048,768]{1,0:T(8,128)(2,1)} %convolution_convert_fusion.2) | data formatting | bytes 6291456
  196.4 1.5 copy-done.2
  197.8 5.7 %convolution_convert_fusion = bf16[768,2048]{1,0:T(8,128)(2,1)} fusion(bf16[512,2048]{1,0:T(8,128)(2,1)} %bitcast.4, f32[512]{0:T(512)S(1)} %reshape.120, f32[512,768]{1,0:T(8,128)} %fusion.6, f32[512,768]{1,0:T(8,128)S(1)} %copy-done.2), kind=kOutput, calls=%fused_computation.1 | convolution fusion | flops 1614938112 | bytes 8390656 | tf_op jit(solution)/shard_map/dot_general | solution.py:36
  203.6 1.1 copy-done.3
  204.7 3.9 %fusion = f32[512,2048]{1,0:T(8,128)S(1)} fusion(bf16[512,768]{1,0:T(8,128)(2,1)S(1)} %copy-done.3, bf16[1,1,2048,768]{3,2,1,0:T(8,128)(2,1)} %all-gather.7.cloned.1.call-done), kind=kOutput, calls=%fused_computation.5 | convolution fusion | flops 1610612736 | bytes 8126464 | tf_op jit(solution)/shard_map/dot_general | solution.py:29
  208.5 1.8 add_convert_fusion
  210.4 50.4 %all_to_all.33 = bf16[32,16,2048]{2,1,0:T(8,128)(2,1)S(1)} all-to-all(bf16[32,16,2048]{2,1,0:T(8,128)(2,1)S(1)} %bitcast.77), channel_id=1, replica_groups=mesh['section'=4,'dp'=2,'expert'=32] {'expert'}, dimensions={0} | all-to-all | bytes 4194304 | tf_op jit(solution)/shard_map/all_to_all | solution.py:120
  261.3 0.9 collective-permute-start
  263.0 8.8 %collective-permute-done = bf16[128,2048]{1,0:T(8,128)(2,1)S(1)} collective-permute-done((bf16[128,2048]{1,0:T(8,128)(2,1)S(1)}, bf16[128,2048]{1,0:T(8,128)(2,1)S(1)}, u32[]{:S(2)}, u32[]{:S(2)}) %collective-permute-start) | collective-permute-done | bytes 524320 | tf_op jit(solution)/shard_map/ppermute | solution.py:9
  271.8 2.6 copy.39
  274.3 2.6 copy.37
  277.0 0.8 copy.43
  (54 shorter events, 5.4 us)
Async XLA Ops:
  7.2 10.9 %copy-start = (bf16[1,128,2048]{2,1,0:T(8,128)(2,1)S(1)}, bf16[1,128,2048]{2,1,0:T(8,128)(2,1)}, u32[]{:S(2)}) copy-start(bf16[1,128,2048]{2,1,0:T(8,128)(2,1)} %param.7) | copy-start | bytes 1572868
  11.1 5.3 %copy-start.5 = (s32[1,128,2]{1,2,0:T(2,128)S(1)}, s32[1,128,2]{1,2,0:T(2,128)}, u32[]{:S(2)}) copy-start(s32[1,128,2]{1,2,0:T(2,128)} %param.9) | copy-start | bytes 3076
  11.1 9.1 %all-to-all-start.2 = ((bf16[2,384,2048]{2,1,0:T(8,128)(2,1)}), bf16[2,384,2048]{2,1,0:T(8,128)(2,1)}, u32[]{:S(2)}, u32[]{:S(2)}) async-start(bf16[2,384,2048]{2,1,0:T(8,128)(2,1)} %pad_maximum_fusion), calls=%async_computation.2 | async-start | bytes 6291456 | tf_op jit(solution)/shard_map/all_to_all | solution.py:102
  20.2 12.4 %copy-start.4 = (bf16[1,128,2048]{2,1,0:T(8,128)(2,1)S(1)}, bf16[1,128,2048]{2,1,0:T(8,128)(2,1)}, u32[]{:S(2)}) copy-start(bf16[1,128,2048]{2,1,0:T(8,128)(2,1)} %param.8) | copy-start | bytes 1572868
  20.2 62.4 %all-to-all-start.3 = ((bf16[32,16,2048]{2,1,0:T(8,128)(2,1)}), bf16[32,16,2048]{2,1,0:T(8,128)(2,1)S(1)}, u32[]{:S(2)}, u32[]{:S(2)}) async-start(bf16[32,16,2048]{2,1,0:T(8,128)(2,1)} %bitcast.8), calls=%async_computation.3 | async-start | bytes 4194304 | tf_op jit(solution)/shard_map/all_to_all | solution.py:70
  31.8 57.7 %all-gather.7.cloned.1.call-start = ((), (), s32[]{:S(2)}) async-start(), calls=%async_computation.11 | async-start | bytes 4718592 | tf_op jit(solution)/shard_map/all_gather | solution.py:99
  82.6 55.9 %all-to-all-start.1 = ((bf16[32,16,2048]{2,1,0:T(8,128)(2,1)}), bf16[32,16,2048]{2,1,0:T(8,128)(2,1)}, u32[]{:S(2)}, u32[]{:S(2)}) async-start(bf16[32,16,2048]{2,1,0:T(8,128)(2,1)} %bitcast.3), calls=%async_computation.1 | async-start | bytes 4194304 | tf_op jit(solution)/shard_map/all_to_all | solution.py:77
  88.7 21.2 %all-gather.5.cloned.1.call-start = ((), (), s32[]{:S(2)}) async-start(), calls=%async_computation.10 | async-start | bytes 4718592 | tf_op jit(solution)/shard_map/all_gather | solution.py:100
  138.5 13.2 %copy-start.6 = (f32[1,128,2]{1,2,0:T(2,128)S(1)}, f32[1,128,2]{1,2,0:T(2,128)}, u32[]{:S(2)}) copy-start(f32[1,128,2]{1,2,0:T(2,128)} %param.10) | copy-start | bytes 3076
  145.7 15.6 %all-to-all-start.5 = ((bf16[32,1,16]{2,1,0:T(2,128)(2,1)}), bf16[32,1,16]{2,1,0:T(2,128)(2,1)S(1)}, u32[]{:S(2)}, u32[]{:S(2)}) async-start(bf16[32,1,16]{2,1,0:T(2,128)(2,1)} %convert_element_type.113), calls=%async_computation.5 | async-start | bytes 32768 | tf_op jit(solution)/shard_map/all_to_all | solution.py:127
  151.6 120.2 %reduce-scatter.12.cloned.1.call-start = ((), (), s32[]{:S(2)}) async-start(), calls=%async_computation.13 | async-start | bytes 4718592
  186.8 87.5 %reduce-scatter.10.cloned.1.call-start = ((), (), s32[]{:S(2)}) async-start(), calls=%async_computation.12 | async-start | bytes 4718592
  196.3 1.5 copy-start.2
  196.3 80.7 %reduce-scatter.8.cloned.1.call-start = ((), (), s32[]{:S(2)}) async-start(), calls=%async_computation.9 | async-start | bytes 4718592 | tf_op jit(solution)/shard_map/reduce_scatter | solution.py:115
  203.5 1.1 copy-start.3
  204.7 3.9 %copy-start.7 = (bf16[1,1,2048,768]{3,2,1,0:T(8,128)(2,1)S(1)}, bf16[1,1,2048,768]{3,2,1,0:T(8,128)(2,1)}, u32[]{:S(2)}) copy-start(bf16[1,1,2048,768]{3,2,1,0:T(8,128)(2,1)} %all-gather.5.cloned.1.call-done) | copy-start | bytes 9437188
  261.3 10.5 %collective-permute-start = (bf16[128,2048]{1,0:T(8,128)(2,1)S(1)}, bf16[128,2048]{1,0:T(8,128)(2,1)S(1)}, u32[]{:S(2)}, u32[]{:S(2)}) collective-permute-start(bf16[128,2048]{1,0:T(8,128)(2,1)S(1)} %convolution_convert_fusion.5), channel_id=1, source_target_pairs={{0,192},{64,0},{128,64},{192,128},{1,193},{65,1},{129,65},{193,129... | collective-permute-start | bytes 1572872 | tf_op jit(solution)/shard_map/ppermute | solution.py:9
  274.3 3.4 %copy-start.1 = (bf16[1,128,2048]{2,1,0:T(8,128)(2,1)S(1)}, bf16[1,128,2048]{2,1,0:T(8,128)(2,1)}, u32[]{:S(2)}) copy-start(bf16[1,128,2048]{2,1,0:T(8,128)(2,1)} %param.7) | copy-start | bytes 1572868
Sparse Core Ops, SparseCore 0:
  34.5 18.5 all-gather.6
  91.3 18.4 all-gather.4
  187.0 10.5 reduce-scatter.11
  200.1 17.5 reduce-scatter.9
  220.6 17.4 reduce-scatter.7
